TPU v7x, 256 devices: a whole 4x4x8 slice. The times are simulated.
256 devices in a mesh: layer: 8 (over z_lo, core), feat: 32 (over x, y, z_hi).
Axes of the slice: x: 4, y: 4, z: 8 (z_hi: 2, z_lo: 4; z = z_hi * 4 + z_lo), core: 2. Of those that a mesh axis runs over, the one named last changes fastest.
Arguments:
- source: bfloat16 [512, 2304], P('feat', 'layer'), may hold values from -6 to 6
- enc_weight: bfloat16 [2304, 32768], P('layer', 'feat'), may hold values from -0.125 to 0.125
- enc_bias: float32 [32768], P('feat'), may hold values from -3 to 3
- dec_weight: bfloat16 [8, 32768, 2304], P('layer', 'feat'), may hold values from -0.03125 to 0.03125
- dec_bias: float32 [8, 2304], P('layer'), may hold values from -3 to 3
- targets: bfloat16 [8, 512, 2304], P('layer', 'feat'), may hold values from -6 to 6
Outputs:
- enc_grad: bfloat16 [2304, 32768], P('layer', 'feat')
- dec_grad: bfloat16 [8, 32768, 2304], P('layer', 'feat')
All inputs are finite; a program needn't handle non-finite values.
Results may differ from a plain program's by a relative error of at most 0.014.
Values may be sent and summed in bfloat16 or wider, within the bound.
A program may use at most 64 MiB of HBM per device.

v0:
```python
import jax
import jax.numpy as jnp
from jax import lax
from jax.sharding import PartitionSpec as P


def body(source, enc_weight, enc_bias, dec_weight, dec_bias, targets):
    source_rows = lax.all_gather(source, "feat", axis=0, tiled=True)
    partial_input = jnp.dot(source_rows, enc_weight, preferred_element_type=jnp.float32)
    preact = lax.psum(partial_input, "layer")
    preact = preact + enc_bias[None, :]
    active = jnp.maximum(preact, 0.0)
    features = (active * active).astype(jnp.bfloat16)
    decoder = dec_weight[0]
    picked = features
    rebuilt = lax.psum_scatter(
        jnp.dot(picked, decoder, preferred_element_type=jnp.float32).astype(jnp.bfloat16),
        "feat",
        scatter_dimension=0,
        tiled=True,
    ).astype(jnp.float32)
    rebuilt = rebuilt + dec_bias[0][None, :]
    residual = (rebuilt - targets[0].astype(jnp.float32)).astype(jnp.bfloat16)
    piece = lax.all_gather(residual, "feat", axis=0, tiled=True)
    picked = features
    weight_total = lax.dot_general(
        picked, piece, (((0,), (0,)), ((), ())), preferred_element_type=jnp.float32
    )
    grad_block = lax.dot_general(
        piece, decoder, (((1,), (1,)), ((), ())), preferred_element_type=jnp.float32
    )
    grad_total = grad_block
    weight_total, grad_total = (weight_total, grad_total)
    summed = lax.psum(grad_total, "layer")
    feat_grad = (2.0 * active * summed).astype(jnp.bfloat16)
    enc_grad = lax.dot_general(
        source_rows, feat_grad, (((0,), (0,)), ((), ())), preferred_element_type=jnp.float32
    ).astype(jnp.bfloat16)
    return (enc_grad, weight_total.astype(jnp.bfloat16)[None])


def solution(mesh):
    placed = (
        P("feat", "layer"),
        P("layer", "feat"),
        P("feat"),
        P("layer", "feat", None),
        P("layer", None),
        P("layer", "feat", None),
    )
    return jax.shard_map(
        body,
        mesh=mesh,
        in_specs=placed,
        out_specs=(P("layer", "feat"), P("layer", "feat", None)),
        check_vma=False,
    )
```

profile of v0, /device:TPU:2, one launch (start us, length us, event | category | flops | bytes accessed | tf_op | source)
XLA Modules:
  0.0 654.4 jit_solution(1544659206685551485)
XLA Ops:
  7.2 0.0 copy-start
  7.2 0.0 all-reduce.3.cloned.1.call-start
  7.2 110.1 %all_gather.6 = bf16[512,288]{1,0:T(8,128)(2,1)S(1)} all-gather(bf16[16,288]{1,0:T(8,128)(2,1)} %param.6), channel_id=1, replica_groups=mesh['layer'=8,'feat'=32] {'feat'}, dimensions={0}, use_global_device_ids=true | all-gather | bytes 304128 | tf_op jit(solution)/shard_map/all_gather | solution.py:8
  117.4 0.0 copy-done
  117.4 2.0 fusion.17
  119.4 0.0 all-reduce.3.cloned.1.call-update
  119.4 0.0 reduce-scatter.2.cloned.1.call-start
  119.5 84.3 %all-reduce.3.cloned.1.call-done = f32[512,1024]{1,0:T(8,128)} async-done(((f32[512,1024]{1,0:T(8,128)}), f32[512,1024]{1,0:T(8,128)}) %all-reduce.3.cloned.1.call-update) | async-done | bytes 2097168 | tf_op jit(solution)/shard_map/psum | solution.py:10
  203.8 0.0 copy-done.4
  203.8 7.0 %fusion.5 = bf16[512,2304]{1,0:T(8,128)(2,1)} fusion(bf16[1,1024,2304]{2,1,0:T(8,128)(2,1)} %param.9, f32[512,1024]{1,0:T(8,128)} %all-reduce.3.cloned.1.call-done, f32[1024]{0:T(1024)S(1)} %copy-done.4), kind=kOutput, calls=%fused_computation.6 | convolution fusion | flops 2419195904 | bytes 9179136 | tf_op jit(solution)/shard_map/dot_general | solution.py:17
  210.8 0.0 reduce-scatter.2.cloned.1.call-update
  210.8 0.0 all-gather.2.cloned.1.call-start
  210.9 0.6 copy-done.3
  211.5 259.3 %reduce-scatter.2.cloned.1.call-done = bf16[16,2304]{1,0:T(8,128)(2,1)} async-done(((bf16[512,2304]{1,0:T(8,128)(2,1)}), bf16[16,2304]{1,0:T(8,128)(2,1)}) %reduce-scatter.2.cloned.1.call-update) | async-done | bytes 73744 | tf_op jit(solution)/shard_map/reduce_scatter | solution.py:16
  470.9 1.5 fusion.12
  472.4 0.0 all-gather.2.cloned.1.call-update
  472.5 0.0 all-reduce.5.cloned.1.call-start
  472.5 90.1 %all-gather.2.cloned.1.call-done = bf16[512,2304]{1,0:T(8,128)(2,1)} async-done(((bf16[16,2304]{1,0:T(8,128)(2,1)}), bf16[512,2304]{1,0:T(8,128)(2,1)}) %all-gather.2.cloned.1.call-update) | async-done | bytes 2359312 | tf_op jit(solution)/shard_map/all_gather | solution.py:24
  562.6 7.1 %fusion.1 = f32[512,1024]{1,0:T(8,128)} fusion(bf16[512,2304]{1,0:T(8,128)(2,1)} %all-gather.2.cloned.1.call-done, bf16[1,1024,2304]{2,1,0:T(8,128)(2,1)} %param.9), kind=kOutput, calls=%fused_computation.2 | convolution fusion | flops 2415919104 | bytes 9175040 | tf_op jit(solution)/shard_map/dot_general | solution.py:29
  569.7 0.0 all-reduce.5.cloned.1.call-update
  569.7 1.6 copy-done.1
  571.3 6.0 fusion
  577.2 67.6 %all-reduce.5.cloned.1.call-done = f32[512,1024]{1,0:T(8,128)} async-done(((f32[512,1024]{1,0:T(8,128)}), f32[512,1024]{1,0:T(8,128)}) %all-reduce.5.cloned.1.call-update) | async-done | bytes 2097168 | tf_op jit(solution)/shard_map/psum | solution.py:34
  644.9 3.0 fusion.8
  (6 shorter events, 0.0 us)
Async XLA Ops:
  7.2 110.2 %copy-start = (bf16[288,1024]{1,0:T(8,128)(2,1)S(1)}, bf16[288,1024]{1,0:T(8,128)(2,1)}, u32[]{:S(2)}) copy-start(bf16[288,1024]{1,0:T(8,128)(2,1)} %param.7) | copy-start | bytes 1769476
  7.2 196.6 %all-reduce.3.cloned.1.call-start = ((), (), s32[]{:S(2)}) async-start(), calls=%async_computation.1 | async-start | bytes 4194304 | tf_op jit(solution)/shard_map/psum | solution.py:10
  117.4 86.4 %copy-start.4 = (f32[1024]{0:T(1024)S(1)}, f32[1024]{0:T(1024)}, u32[]{:S(2)}) copy-start(f32[1024]{0:T(1024)} %param.8) | copy-start | bytes 12292
  119.4 351.5 %reduce-scatter.2.cloned.1.call-start = ((), (), s32[]{:S(2)}) async-start(), calls=%async_computation.2 | async-start | bytes 2433024 | tf_op jit(solution)/shard_map/reduce_scatter | solution.py:16
  210.8 0.7 copy-start.3
  210.8 260.1 %copy-start.2 = (bf16[1,16,2304]{2,1,0:T(8,128)(2,1)S(1)}, bf16[1,16,2304]{2,1,0:T(8,128)(2,1)}, u32[]{:S(2)}) copy-start(bf16[1,16,2304]{2,1,0:T(8,128)(2,1)} %param.11) | copy-start | bytes 221188
  210.8 351.8 %all-gather.2.cloned.1.call-start = ((), (), s32[]{:S(2)}) async-start(), calls=%async_computation.3 | async-start | bytes 2433024 | tf_op jit(solution)/shard_map/all_gather | solution.py:24
  472.5 172.4 %all-reduce.5.cloned.1.call-start = ((), (), s32[]{:S(2)}) async-start(), calls=%async_computation.4 | async-start | bytes 4194304 | tf_op jit(solution)/shard_map/psum | solution.py:34
  569.7 1.6 copy-start.1
Sparse Core Ops, SparseCore 0:
  119.5 84.2 all-reduce.2
  211.0 259.8 reduce-scatter.1
  474.9 87.7 all-gather.1
  569.8 75.0 all-reduce.4
where the time goes:
time: 655 us; the launch traced here: 654 us
  waiting for transfers between devices  501 us (76%)
  blocking collectives  110 us (17%)
  matrix products  25.1 us (4%)
  between operations  13.8 us (2%)
    reduce_scatter x1, waiting for transfers between devices, body(): lax.psum_scatter(jnp.dot(picked, decoder, preferred_element_type=jnp.floa...  259 us
    all_gather x1, blocking collectives, body(): source_rows = lax.all_gather(source, 'feat', axis=0, tiled=True)  110 us
    all_gather x1, waiting for transfers between devices, body(): piece = lax.all_gather(residual, 'feat', axis=0, tiled=True)  90.1 us
    psum x1, waiting for transfers between devices, body(): preact = lax.psum(partial_input, 'layer')  84.3 us
    psum x1, waiting for transfers between devices, body(): summed = lax.psum(grad_total, 'layer')  67.6 us
  transfers between devices with their start and end apart: 4, of which 4 were waited for; matrix products, arithmetic and copies ran while one was open for 1% of the time, Pallas kernels for 0%

commit v1 on v0

--- a/solution.py
+++ b/solution.py
@@ -5,7 +5,9 @@
 
 
 def body(source, enc_weight, enc_bias, dec_weight, dec_bias, targets):
-    source_rows = lax.all_gather(source, "feat", axis=0, tiled=True)
+    source_rows = jnp.concatenate(
+        lax.all_to_all(jnp.stack([source] * lax.axis_size("feat")), "feat", 0, 0), axis=0
+    )
     partial_input = jnp.dot(source_rows, enc_weight, preferred_element_type=jnp.float32)
     preact = lax.psum(partial_input, "layer")
     preact = preact + enc_bias[None, :]

time: 655 us -> 567 us (0.87)
  blocking collectives: 110 us -> 27.5 us
    all_gather x1 -> x0, blocking collectives: 110 us -> none  [body(): source_rows = lax.all_gather(source, 'feat', axis=0, tiled=True)]
    all_to_all x0 -> x1, blocking collectives: none -> 27.5 us  [body(): lax.all_to_all(jnp.stack([source] * lax.axis_size('feat')), 'feat', 0, 0)]
where the time goes in v1:
time: 567 us
  waiting for transfers between devices  496 us (87%)
  blocking collectives  27.5 us (5%)
  matrix products  25.1 us (4%)
  between operations  13.8 us (2%)
    reduce_scatter x1, waiting for transfers between devices, body(): lax.psum_scatter(jnp.dot(picked, decoder, preferred_element_type=jnp.floa...  259 us
    all_gather x1, waiting for transfers between devices, body(): piece = lax.all_gather(residual, 'feat', axis=0, tiled=True)  90.2 us
    psum x1, waiting for transfers between devices, body(): preact = lax.psum(partial_input, 'layer')  78.9 us
    psum x1, waiting for transfers between devices, body(): summed = lax.psum(grad_total, 'layer')  67.6 us
    all_to_all x1, blocking collectives, body(): lax.all_to_all(jnp.stack([source] * lax.axis_size('feat')), 'feat', 0, 0)  27.5 us
  transfers between devices with their start and end apart: 4, of which 4 were waited for; matrix products, arithmetic and copies ran while one was open for 1% of the time, Pallas kernels for 0%

profile of v1, /device:TPU:2, one launch (start us, length us, event | category | flops | bytes accessed | tf_op | source)
XLA Modules:
  0.0 567.1 jit_solution(16231936883823019276)
XLA Ops:
  7.2 0.0 copy-start
  7.2 0.0 all-reduce.3.cloned.1.call-start
  7.2 0.8 stack.2
  8.0 27.5 %all_to_all.5 = bf16[32,16,288]{2,1,0:T(8,128)(2,1)S(1)} all-to-all(bf16[32,16,288]{2,1,0:T(8,128)(2,1)S(1)} %stack.2), channel_id=1, replica_groups=mesh['layer'=8,'feat'=32] {'feat'}, dimensions={0} | all-to-all | bytes 589824 | tf_op jit(solution)/shard_map/all_to_all | solution.py:9
  35.5 0.0 copy-done
  35.5 2.0 fusion.17
  37.5 0.0 all-reduce.3.cloned.1.call-update
  37.6 0.0 reduce-scatter.2.cloned.1.call-start
  37.6 78.9 %all-reduce.3.cloned.1.call-done = f32[512,1024]{1,0:T(8,128)} async-done(((f32[512,1024]{1,0:T(8,128)}), f32[512,1024]{1,0:T(8,128)}) %all-reduce.3.cloned.1.call-update) | async-done | bytes 2097168 | tf_op jit(solution)/shard_map/psum | solution.py:12
  116.5 7.0 %fusion.5 = bf16[512,2304]{1,0:T(8,128)(2,1)} fusion(bf16[1,1024,2304]{2,1,0:T(8,128)(2,1)} %param.9, f32[512,1024]{1,0:T(8,128)} %all-reduce.3.cloned.1.call-done, f32[1024]{0:T(1024)S(1)} %copy-done.4), kind=kOutput, calls=%fused_computation.6 | convolution fusion | flops 2419195904 | bytes 9179136 | tf_op jit(solution)/shard_map/dot_general | solution.py:19
  123.5 0.0 reduce-scatter.2.cloned.1.call-update
  123.5 0.0 all-gather.2.cloned.1.call-start
  123.6 0.6 copy-done.3
  124.2 259.3 %reduce-scatter.2.cloned.1.call-done = bf16[16,2304]{1,0:T(8,128)(2,1)} async-done(((bf16[512,2304]{1,0:T(8,128)(2,1)}), bf16[16,2304]{1,0:T(8,128)(2,1)}) %reduce-scatter.2.cloned.1.call-update) | async-done | bytes 73744 | tf_op jit(solution)/shard_map/reduce_scatter | solution.py:18
  383.5 1.5 fusion.12
  385.1 0.0 all-gather.2.cloned.1.call-update
  385.1 0.0 all-reduce.5.cloned.1.call-start
  385.1 90.2 %all-gather.2.cloned.1.call-done = bf16[512,2304]{1,0:T(8,128)(2,1)} async-done(((bf16[16,2304]{1,0:T(8,128)(2,1)}), bf16[512,2304]{1,0:T(8,128)(2,1)}) %all-gather.2.cloned.1.call-update) | async-done | bytes 2359312 | tf_op jit(solution)/shard_map/all_gather | solution.py:26
  475.3 7.1 %fusion.1 = f32[512,1024]{1,0:T(8,128)} fusion(bf16[512,2304]{1,0:T(8,128)(2,1)} %all-gather.2.cloned.1.call-done, bf16[1,1024,2304]{2,1,0:T(8,128)(2,1)} %param.9), kind=kOutput, calls=%fused_computation.2 | convolution fusion | flops 2415919104 | bytes 9175040 | tf_op jit(solution)/shard_map/dot_general | solution.py:31
  482.4 0.0 all-reduce.5.cloned.1.call-update
  482.4 1.6 copy-done.1
  484.0 6.0 %fusion = bf16[1,1024,2304]{2,1,0:T(8,128)(2,1)} fusion(bf16[512,2304]{1,0:T(8,128)(2,1)} %all-gather.2.cloned.1.call-done, f32[512,1024]{1,0:T(8,128)S(1)} %copy-done.1, f32[1024]{0:T(1024)S(1)} %copy-done.4), kind=kOutput, calls=%fused_computation.1 | convolution fusion | flops 2420375552 | bytes 9179136 | tf_op jit(solution)/shard_map/dot_general | solution.py:28
  489.9 67.6 %all-reduce.5.cloned.1.call-done = f32[512,1024]{1,0:T(8,128)} async-done(((f32[512,1024]{1,0:T(8,128)}), f32[512,1024]{1,0:T(8,128)}) %all-reduce.5.cloned.1.call-update) | async-done | bytes 2097168 | tf_op jit(solution)/shard_map/psum | solution.py:36
  557.5 3.0 fusion.8
  (7 shorter events, 0.0 us)
Async XLA Ops:
  7.2 28.3 %copy-start = (bf16[288,1024]{1,0:T(8,128)(2,1)S(1)}, bf16[288,1024]{1,0:T(8,128)(2,1)}, u32[]{:S(2)}) copy-start(bf16[288,1024]{1,0:T(8,128)(2,1)} %param.7) | copy-start | bytes 1769476
  7.2 109.3 %all-reduce.3.cloned.1.call-start = ((), (), s32[]{:S(2)}) async-start(), calls=%async_computation.2 | async-start | bytes 4194304 | tf_op jit(solution)/shard_map/psum | solution.py:12
  35.5 81.0 %copy-start.4 = (f32[1024]{0:T(1024)S(1)}, f32[1024]{0:T(1024)}, u32[]{:S(2)}) copy-start(f32[1024]{0:T(1024)} %param.8) | copy-start | bytes 12292
  37.6 345.9 %reduce-scatter.2.cloned.1.call-start = ((), (), s32[]{:S(2)}) async-start(), calls=%async_computation.3 | async-start | bytes 2433024 | tf_op jit(solution)/shard_map/reduce_scatter | solution.py:18
  123.5 0.7 copy-start.3
  123.5 260.0 %copy-start.2 = (bf16[1,16,2304]{2,1,0:T(8,128)(2,1)S(1)}, bf16[1,16,2304]{2,1,0:T(8,128)(2,1)}, u32[]{:S(2)}) copy-start(bf16[1,16,2304]{2,1,0:T(8,128)(2,1)} %param.11) | copy-start | bytes 221188
  123.5 351.8 %all-gather.2.cloned.1.call-start = ((), (), s32[]{:S(2)}) async-start(), calls=%async_computation.4 | async-start | bytes 2433024 | tf_op jit(solution)/shard_map/all_gather | solution.py:26
  385.1 172.5 %all-reduce.5.cloned.1.call-start = ((), (), s32[]{:S(2)}) async-start(), calls=%async_computation.5 | async-start | bytes 4194304 | tf_op jit(solution)/shard_map/psum | solution.py:36
  482.4 1.6 copy-start.1
Sparse Core Ops, SparseCore 0:
  37.7 78.7 all-reduce.2
  123.6 259.8 reduce-scatter.1
  387.5 87.7 all-gather.1
  482.5 74.9 all-reduce.4

commit v2 on v0

--- a/solution.py
+++ b/solution.py
@@ -7,7 +7,7 @@
 def body(source, enc_weight, enc_bias, dec_weight, dec_bias, targets):
     source_rows = lax.all_gather(source, "feat", axis=0, tiled=True)
     partial_input = jnp.dot(source_rows, enc_weight, preferred_element_type=jnp.float32)
-    preact = lax.psum(partial_input, "layer")
+    preact = jnp.sum(lax.all_gather(partial_input, "layer"), axis=0)
     preact = preact + enc_bias[None, :]
     active = jnp.maximum(preact, 0.0)
     features = (active * active).astype(jnp.bfloat16)

time: 655 us -> 753 us (1.15)
  waiting for transfers between devices: 501 us -> 594 us
  other arithmetic: 1.58 us -> 9.53 us
    all_gather x0 -> x1, waiting for transfers between devices: none -> 177 us  [body(): preact = jnp.sum(lax.all_gather(partial_input, 'layer'), axis=0)]
    psum x1 -> x0, waiting for transfers between devices: 84.3 us -> none  [body(): preact = lax.psum(partial_input, 'layer')]
    reduce_sum x0 -> x1, other arithmetic: none -> 7.96 us  [body(): preact = jnp.sum(lax.all_gather(partial_input, 'layer'), axis=0)]
where the time goes in v2:
time: 753 us
  waiting for transfers between devices  594 us (79%)
  blocking collectives  110 us (15%)
  matrix products  24.2 us (3%)
  between operations  13.8 us (2%)
  other arithmetic  9.53 us (1%)
    reduce_scatter x1, waiting for transfers between devices, body(): lax.psum_scatter(jnp.dot(picked, decoder, preferred_element_type=jnp.floa...  258 us
    all_gather x1, waiting for transfers between devices, body(): preact = jnp.sum(lax.all_gather(partial_input, 'layer'), axis=0)  177 us
    all_gather x1, blocking collectives, body(): source_rows = lax.all_gather(source, 'feat', axis=0, tiled=True)  110 us
    all_gather x1, waiting for transfers between devices, body(): piece = lax.all_gather(residual, 'feat', axis=0, tiled=True)  90.2 us
    psum x1, waiting for transfers between devices, body(): summed = lax.psum(grad_total, 'layer')  69.2 us
  transfers between devices with their start and end apart: 4, of which 4 were waited for; matrix products, arithmetic and copies ran while one was open for 1% of the time, Pallas kernels for 0%

profile of v2, /device:TPU:2, one launch (start us, length us, event | category | flops | bytes accessed | tf_op | source)
XLA Modules:
  0.0 752.9 jit_solution(3608681027071908483)
XLA Ops:
  7.2 0.0 copy-start
  7.2 0.0 all-gather.6.cloned.1.call-start
  7.2 110.1 %all_gather.12 = bf16[512,288]{1,0:T(8,128)(2,1)S(1)} all-gather(bf16[16,288]{1,0:T(8,128)(2,1)} %param.6), channel_id=1, replica_groups=mesh['layer'=8,'feat'=32] {'feat'}, dimensions={0}, use_global_device_ids=true | all-gather | bytes 304128 | tf_op jit(solution)/shard_map/all_gather | solution.py:8
  117.4 0.0 copy-done
  117.4 2.0 fusion.17
  119.4 0.0 all-gather.6.cloned.1.call-update
  119.4 0.0 reduce-scatter.2.cloned.1.call-start
  119.5 177.0 %all-gather.6.cloned.1.call-done = f32[4096,1024]{1,0:T(8,128)} async-done(((f32[512,1024]{1,0:T(8,128)}), f32[4096,1024]{1,0:T(8,128)}) %all-gather.6.cloned.1.call-update) | async-done | bytes 16777232 | tf_op jit(solution)/shard_map/all_gather | solution.py:10
  296.5 8.0 %reduce_sum.9 = f32[512,1024]{1,0:T(8,128)S(1)} reduce(f32[8,512,1024]{2,1,0:T(8,128)} %bitcast.20, f32[]{:T(128)} %constant.2.clone.1), dimensions={0}, to_apply=%region_0.0 | reduce | flops 3670016 | bytes 18874372 | tf_op jit(solution)/shard_map/reduce_sum | solution.py:10
  304.5 6.2 fusion.5
  310.7 0.0 reduce-scatter.2.cloned.1.call-update
  310.7 0.0 all-gather.4.cloned.1.call-start
  310.7 0.6 copy-done.2
  311.4 258.0 %reduce-scatter.2.cloned.1.call-done = bf16[16,2304]{1,0:T(8,128)(2,1)} async-done(((bf16[512,2304]{1,0:T(8,128)(2,1)}), bf16[16,2304]{1,0:T(8,128)(2,1)}) %reduce-scatter.2.cloned.1.call-update) | async-done | bytes 73744 | tf_op jit(solution)/shard_map/reduce_scatter | solution.py:16
  569.4 0.0 copy-done.1
  569.4 1.5 fusion.12
  570.9 0.0 all-gather.4.cloned.1.call-update
  570.9 0.0 all-reduce.2.cloned.1.call-start
  571.0 90.2 %all-gather.4.cloned.1.call-done = bf16[512,2304]{1,0:T(8,128)(2,1)} async-done(((bf16[16,2304]{1,0:T(8,128)(2,1)}), bf16[512,2304]{1,0:T(8,128)(2,1)}) %all-gather.4.cloned.1.call-update) | async-done | bytes 2359312 | tf_op jit(solution)/shard_map/all_gather | solution.py:24
  661.1 7.0 fusion.1
  668.2 0.0 all-reduce.2.cloned.1.call-update
  668.2 6.0 fusion
  674.2 69.2 %all-reduce.2.cloned.1.call-done = f32[512,1024]{1,0:T(8,128)} async-done(((f32[512,1024]{1,0:T(8,128)}), f32[512,1024]{1,0:T(8,128)}) %all-reduce.2.cloned.1.call-update) | async-done | bytes 2097168 | tf_op jit(solution)/shard_map/psum | solution.py:34
  743.4 3.0 fusion.8
  (5 shorter events, 0.0 us)
Async XLA Ops:
  7.2 110.2 %copy-start = (bf16[288,1024]{1,0:T(8,128)(2,1)S(1)}, bf16[288,1024]{1,0:T(8,128)(2,1)}, u32[]{:S(2)}) copy-start(bf16[288,1024]{1,0:T(8,128)(2,1)} %param.7) | copy-start | bytes 1769476
  7.2 289.3 %all-gather.6.cloned.1.call-start = ((), (), s32[]{:S(2)}) async-start(), calls=%async_computation.4 | async-start | bytes 18874368 | tf_op jit(solution)/shard_map/all_gather | solution.py:10
  119.4 449.9 %reduce-scatter.2.cloned.1.call-start = ((), (), s32[]{:S(2)}) async-start(), calls=%async_computation.1 | async-start | bytes 2433024 | tf_op jit(solution)/shard_map/reduce_scatter | solution.py:16
  296.5 8.0 %copy-start.3 = (f32[1024]{0:T(1024)S(1)}, f32[1024]{0:T(1024)}, u32[]{:S(2)}) copy-start(f32[1024]{0:T(1024)} %param.8) | copy-start | bytes 12292
  310.7 0.7 copy-start.2
  310.7 258.7 %copy-start.1 = (bf16[1,16,2304]{2,1,0:T(8,128)(2,1)S(1)}, bf16[1,16,2304]{2,1,0:T(8,128)(2,1)}, u32[]{:S(2)}) copy-start(bf16[1,16,2304]{2,1,0:T(8,128)(2,1)} %param.11) | copy-start | bytes 221188
  310.7 350.5 %all-gather.4.cloned.1.call-start = ((), (), s32[]{:S(2)}) async-start(), calls=%async_computation.2 | async-start | bytes 2433024 | tf_op jit(solution)/shard_map/all_gather | solution.py:24
  570.9 172.4 %all-reduce.2.cloned.1.call-start = ((), (), s32[]{:S(2)}) async-start(), calls=%async_computation.3 | async-start | bytes 4194304 | tf_op jit(solution)/shard_map/psum | solution.py:34
Sparse Core Ops, SparseCore 0:
  119.5 176.9 all-gather.5
  310.8 258.5 reduce-scatter.1
  573.3 87.7 all-gather.3
  668.3 74.9 all-reduce.1
